TPU v7x, 32 devices: a whole 2x2x4 slice. The times are simulated.
32 devices in a mesh: row: 8 (over y, x, core), col: 4 (over z).
Axes of the slice: x: 2, y: 2, z: 4, core: 2. Of those that a mesh axis runs over, the one named last changes fastest.
Arguments:
- in_map: bfloat16 [128, 128, 256], P('row', 'col'), may hold values from -6 to 6
- tile_w: bfloat16 [3, 3, 256, 256], replicated, may hold values from -0.125 to 0.125
- head_w1: bfloat16 [3, 3, 256, 256], replicated, may hold values from -0.125 to 0.125
- head_w2: bfloat16 [3, 3, 256, 256], replicated, may hold values from -0.125 to 0.125
- box_row: int32 [64, 4], P('row', 'col'), may hold values from 0 to 2
- box_col: int32 [64, 4], P('row', 'col'), may hold values from 0 to 18
- box_target: int32 [64, 4], P('row', 'col'), may hold values from -1 to 15, as said below
- head_cot: bfloat16 [32, 4, 14, 14, 256], P('row', 'col'), may hold values from -6 to 6
Outputs:
- grad_map: bfloat16 [128, 128, 256], P('row', 'col')
- grad_w1: float32 [3, 3, 256, 256], replicated
- grad_w2: float32 [3, 3, 256, 256], replicated
Inputs may be any that keep to these rules, and one draw needn't show every extreme that they name: `box_target`: within each row r of tiles, every head slot d * 4 + h (d below 4, h below 4) is named by exactly one tile slot, and empty slots hold -1. A tile names at most 2 head slots of one device, so it holds at most 8 boxes; in every row of tiles one tile holds 8 boxes, 2 for each device of the row.
All inputs are finite; a program needn't handle non-finite values.
Results may differ from a plain program's by a relative error of at most 0.012.
Values may be sent and summed in bfloat16 or wider, within the bound.
No kernel may reach another device: no remote copies, remote signals or barrier semaphores. Data moves between devices by JAX's collectives and lax.ppermute only.
A program may use at most 64 MiB of HBM per device.

v0:
```python
import math
import jax
import jax.numpy as jnp
from jax import lax
from jax.sharding import PartitionSpec as P

LAYOUT = ("NHWC", "HWIO", "NHWC")


def padded_2(shard, sides, width):
    for axis, dim in sides:
        size, length = (lax.axis_size(axis), shard.shape[dim])
        up = [(i, (i + 1) % size) for i in range(size - 1)]
        down = [(j, i) for i, j in up]
        last = lax.slice_in_dim(shard, length - width, length, axis=dim)
        leading = lax.slice_in_dim(shard, 0, width, axis=dim)
        before = lax.ppermute(last, axis, up)
        after = lax.ppermute(leading, axis, down)
        shard = jnp.concatenate([before, shard, after], axis=dim)
    return shard


def conv_pad(inputs, kernel, margin):
    return lax.conv_general_dilated(
        inputs,
        kernel,
        (1, 1),
        ((margin, margin), (margin, margin)),
        dimension_numbers=LAYOUT,
        preferred_element_type=jnp.float32,
    )


def flip_weights(kernel):
    return jnp.transpose(jnp.flip(kernel, (0, 1)), (0, 1, 3, 2))


def silu_slope(values):
    sigma = jax.nn.sigmoid(values)
    return sigma * (1.0 + values * (1.0 - sigma))


def weight_grad(inputs, deltas):
    channels = inputs.shape[-1]
    box_side = inputs.shape[1]
    padded = jnp.pad(inputs, ((0, 0), (1, 1), (1, 1), (0, 0)))
    flat_delta = deltas.reshape(-1, channels)
    blocks = []
    for shift_y in range(3):
        for shift_x in range(3):
            window = padded[
                :, shift_y : shift_y + box_side, shift_x : shift_x + box_side, :
            ].reshape(-1, channels)
            blocks.append(
                lax.dot_general(
                    window, flat_delta, (((0,), (0,)), ((), ())), preferred_element_type=jnp.float32
                )
            )
    return jnp.stack(blocks).reshape(3, 3, channels, channels)


def pick_rows(table, values):
    flat = values.reshape(values.shape[0], -1)
    return jnp.dot(table, flat, preferred_element_type=jnp.float32).astype(jnp.bfloat16)


def pick_back(table, values):
    return lax.dot_general(
        table, values, (((0,), (0,)), ((), ())), preferred_element_type=jnp.float32
    ).astype(jnp.bfloat16)


def body(in_map, tile_w, head_w1, head_w2, box_row, box_col, box_target, head_cot):
    tile_rows, tile_cols, channels = in_map.shape
    head_count = head_cot.shape[0]
    box_side = head_cot.shape[2]
    slot_count = box_target.shape[0]
    columns = lax.axis_size("col")
    capacity = slot_count // columns
    pair_count = columns * capacity
    padded = padded_2(in_map, (("row", 0), ("col", 1)), 1)
    preact = conv_pad(padded[None], tile_w, 0)[0]
    target = box_target[:, 0]
    occupied = target >= 0
    dest_col = jnp.where(occupied, target // head_count, 0)
    head_slot = jnp.where(occupied, target % head_count, 0)
    slot_ids = jnp.arange(slot_count, dtype=jnp.int32)
    same_dest = (dest_col[:, None] == dest_col[None, :]) & occupied[None, :]
    placing = jnp.sum(same_dest & (slot_ids[None, :] < slot_ids[:, None]), axis=1)
    pair_slot = dest_col * capacity + placing
    pair_ids = jnp.arange(pair_count, dtype=jnp.int32)
    send_map = ((pair_slot[None, :] == pair_ids[:, None]) & occupied[None, :]).astype(jnp.bfloat16)
    head_ids = jnp.arange(head_count, dtype=jnp.int32)
    head_hot = ((head_slot[:, None] == head_ids[None, :]) & occupied[:, None]).astype(jnp.bfloat16)
    pair_head = (
        jnp.dot(send_map, head_hot, preferred_element_type=jnp.float32)
        .astype(jnp.bfloat16)
        .reshape(columns, capacity, head_count)
    )
    top_row = box_row[:, 0]
    left_col = box_col[:, 0]
    zero_index = jnp.zeros((), jnp.int32)
    window = box_side + 2
    windows = jax.vmap(
        lambda y, x: lax.dynamic_slice(padded, (y, x, zero_index), (window, window, channels))
    )(top_row, left_col)
    outgoing = pick_rows(send_map, windows).reshape(columns, capacity, window, window, channels)
    arrived, arrived_head = (
        lax.all_to_all(outgoing, "col", split_axis=0, concat_axis=0, tiled=True),
        lax.all_to_all(pair_head, "col", split_axis=0, concat_axis=0, tiled=True),
    )
    arrived_head = arrived_head.reshape(pair_count, head_count)
    gathered = pick_back(arrived_head, arrived.reshape(pair_count, -1)).reshape(
        head_count, window, window, channels
    )
    box_input = jax.nn.silu(conv_pad(gathered, tile_w, 0)).astype(jnp.bfloat16)
    factor = 1.0 / math.sqrt(lax.axis_size("row") * columns * head_count * box_side * box_side)
    cotangent = head_cot[:, 0]
    pre_one = conv_pad(box_input, head_w1, 1)
    hidden = jax.nn.silu(pre_one).astype(jnp.bfloat16)
    pre_two = conv_pad(hidden, head_w2, 1)
    delta_two = (cotangent.astype(jnp.float32) * silu_slope(pre_two)).astype(jnp.bfloat16)
    second_local = weight_grad(hidden, delta_two)
    delta_one = (conv_pad(delta_two, flip_weights(head_w2), 1) * silu_slope(pre_one)).astype(
        jnp.bfloat16
    )
    box_grads = conv_pad(delta_one, flip_weights(head_w1), 1).astype(jnp.bfloat16)
    sent_back = pick_rows(arrived_head, box_grads).reshape(
        columns, capacity, box_side, box_side, channels
    )
    returned = lax.all_to_all(sent_back, "col", split_axis=0, concat_axis=0, tiled=True)
    slot_grads = pick_back(send_map, returned.reshape(pair_count, -1)).reshape(
        slot_count, box_side, box_side, channels
    )
    first_local = weight_grad(box_input, delta_one)
    first_sum, second_sum = lax.psum((first_local, second_local), ("row", "col"))

    def add_box(slot, running):
        current = lax.dynamic_slice(
            running, (top_row[slot], left_col[slot], zero_index), (box_side, box_side, channels)
        )
        return lax.dynamic_update_slice(
            running,
            current + slot_grads[slot].astype(jnp.float32),
            (top_row[slot], left_col[slot], zero_index),
        )

    box_total = lax.fori_loop(
        0, slot_count, add_box, jnp.zeros((tile_rows, tile_cols, channels), jnp.float32)
    )
    delta_map = (box_total * silu_slope(preact)).astype(jnp.bfloat16)
    delta_rim = padded_2(delta_map, (("row", 0), ("col", 1)), 1)
    grad_map = conv_pad(delta_rim[None], flip_weights(tile_w), 0)[0].astype(jnp.bfloat16)
    return (grad_map, first_sum * factor, second_sum * factor)


def solution(mesh):
    in_specs = (
        P("row", "col", None),
        P(),
        P(),
        P(),
        P("row", "col"),
        P("row", "col"),
        P("row", "col"),
        P("row", "col", None, None, None),
    )
    out_specs = (P("row", "col", None), P(), P())
    return jax.shard_map(body, mesh=mesh, in_specs=in_specs, out_specs=out_specs, check_vma=False)
```

profile of v0, /device:TPU:0, one launch (start us, length us, event | category | flops | bytes accessed | tf_op | source)
XLA Modules:
  0.0 296.8 jit_solution(2329614647910186350)
XLA Ops:
  8.0 1.3 collective-permute-start.1
  9.3 3.0 %collective-permute-start = (bf16[1,32,256]{2,1,0:T(8,128)(2,1)S(1)}, bf16[1,32,256]{2,1,0:T(8,128)(2,1)S(1)}, u32[]{:S(2)}, u32[]{:S(2)}) collective-permute-start(bf16[1,32,256]{2,1,0:T(8,128)(2,1)S(1)} %get-tuple-element.174), channel_id=1, source_target_pairs={{0,4},{4,8},{8,12},{12,16},{16,20},{20,24},{24,28},{1,5},{5,9},{9,... | collective-permute-start | bytes 49160 | tf_op jit(solution)/shard_map/ppermute | solution.py:17
  16.9 5.0 %collective-permute-start.2 = (bf16[18,1,256]{2,1,0:T(2,128)(2,1)S(1)}, bf16[18,1,256]{2,1,0:T(2,128)(2,1)S(1)}, u32[]{:S(2)}, u32[]{:S(2)}) collective-permute-start(bf16[18,1,256]{2,1,0:T(2,128)(2,1)S(1)} %get-tuple-element.169), channel_id=1, source_target_pairs={{0,1},{1,2},{2,3},{4,5},{5,6},{6,7},{8,9},{9,10},{10,11},{12,13},{... | collective-permute-start | bytes 27656 | tf_op jit(solution)/shard_map/ppermute | solution.py:17
  21.9 1.3 collective-permute-start.3
  23.3 4.3 %collective-permute-done.3 = bf16[18,1,256]{2,1,0:T(2,128)(2,1)S(1)} collective-permute-done((bf16[18,1,256]{2,1,0:T(2,128)(2,1)S(1)}, bf16[18,1,256]{2,1,0:T(2,128)(2,1)S(1)}, u32[]{:S(2)}, u32[]{:S(2)}) %collective-permute-start.3) | collective-permute-done | bytes 9248 | tf_op jit(solution)/shard_map/ppermute | solution.py:18
  27.8 20.0 %while.15 = (s32[]{:T(128)}, bf16[18,34,256]{2,1,0:T(8,128)(2,1)S(1)}, s32[8,3]{0,1:T(4,128)S(1)}, bf16[8,16,16,256]{3,2,1,0:T(8,128)(2,1)}, s32[]{:T(128)}) while((s32[]{:T(128)}, bf16[18,34,256]{2,1,0:T(8,128)(2,1)S(1)}, s32[8,3]{0,1:T(4,128)S(1)}, bf16[8,16,16,256]{3,2,1,0:T(8,128)(2,1)}, s32[]{:T(128)}) %tuple.64), condition=%wide.while_cond, body=%wide.while_body.sunk | while | flops 2 | bytes 263285 | solution.py:105
  28.4 1.9 bitcast_dynamic-update-slice_fusion.2
  30.9 1.9 bitcast_dynamic-update-slice_fusion.2
  33.4 1.9 bitcast_dynamic-update-slice_fusion.2
  35.9 1.9 bitcast_dynamic-update-slice_fusion.2
  38.4 1.9 bitcast_dynamic-update-slice_fusion.2
  40.9 1.9 bitcast_dynamic-update-slice_fusion.2
  43.4 1.9 bitcast_dynamic-update-slice_fusion.2
  45.9 1.9 bitcast_dynamic-update-slice_fusion.2
  47.8 1.8 copy.157
  50.0 1.2 copy.158
  51.2 4.0 %all-to-all-start.1 = ((bf16[4,2,16,16,256]{4,3,2,1,0:T(8,128)(2,1)}), bf16[4,2,16,16,256]{4,3,2,1,0:T(8,128)(2,1)S(1)}, u32[]{:S(2)}, u32[]{:S(2)}) async-start(bf16[4,2,16,16,256]{4,3,2,1,0:T(8,128)(2,1)} %bitcast.140), calls=%async_computation.1 | async-start | bytes 2097152 | tf_op jit(solution)/shard_map/all_to_all | solution.py:109
  57.3 1.1 copy.111
  58.4 22.7 %all-to-all-done.1 = bf16[4,2,16,16,256]{4,3,2,1,0:T(8,128)(2,1)S(1)} async-done(((bf16[4,2,16,16,256]{4,3,2,1,0:T(8,128)(2,1)}), bf16[4,2,16,16,256]{4,3,2,1,0:T(8,128)(2,1)S(1)}, u32[]{:S(2)}, u32[]{:S(2)}) %all-to-all-start.1) | async-done | bytes 1048608 | tf_op jit(solution)/shard_map/all_to_all | solution.py:109
  81.0 3.4 %all-to-all-start = ((bf16[4,2,4]{2,1,0:T(2,128)(2,1)}), bf16[4,2,4]{2,1,0:T(2,128)(2,1)S(1)}, u32[]{:S(2)}, u32[]{:S(2)}) async-start(bf16[4,2,4]{2,1,0:T(2,128)(2,1)} %bitcast.9), calls=%async_computation | async-start | bytes 4096 | tf_op jit(solution)/shard_map/all_to_all | solution.py:110
  84.9 4.8 %all-to-all-done = bf16[4,2,4]{2,1,0:T(2,128)(2,1)S(1)} async-done(((bf16[4,2,4]{2,1,0:T(2,128)(2,1)}), bf16[4,2,4]{2,1,0:T(2,128)(2,1)S(1)}, u32[]{:S(2)}, u32[]{:S(2)}) %all-to-all-start) | async-done | bytes 96 | tf_op jit(solution)/shard_map/all_to_all | solution.py:110
  90.9 1.3 multiply_convert_fusion.1
  93.4 1.2 fusion.43
  94.7 1.1 select_bitcast_fusion.1
  96.4 1.3 add_multiply_fusion
  99.1 1.2 fusion.62
  101.6 2.9 fusion.9
  106.2 2.3 copy.120
  108.4 1.2 reshape.164
  111.4 2.5 convolution_convert_fusion.4
  116.3 1.8 copy.105
  118.1 3.5 %all-to-all-start.2 = ((bf16[4,2,14,14,256]{4,1,3,2,0:T(2,128)(2,1)}), bf16[4,2,14,14,256]{4,1,3,2,0:T(2,128)(2,1)S(1)}, u32[]{:S(2)}, u32[]{:S(2)}) async-start(bf16[4,2,14,14,256]{4,1,3,2,0:T(2,128)(2,1)} %copy.105), calls=%async_computation.2 | async-start | bytes 1605632 | tf_op jit(solution)/shard_map/all_to_all | solution.py:131
  121.6 1.4 fusion.28
  130.5 1.1 fusion.17
  134.0 1.3 fusion.14
  136.5 1.1 fusion.12
  137.6 1.1 fusion.11
  138.6 1.8 all-to-all-done.2
  141.9 45.4 %while.14 = (s32[]{:T(128)}, f32[16,32,256]{2,0,1:T(8,128)S(1)}, s32[8]{0:T(128)S(1)}, s32[8]{0:T(128)S(1)}, bf16[8,14,14,256]{3,2,1,0:T(8,128)(2,1)S(1)}, /*index=5*/s32[]{:T(128)}, s32[]{:T(128)}, s32[]{:T(128)}, s32[]{:T(128)}) while((s32[]{:T(128)}, f32[16,32,256]{2,0,1:T(8,128)S(1)}, s32[8]{0:T(128)S(1)}, s32[8]{0:T(128)S(1)}, ...), condition=%wide.region_2.3_spmd, body=%wide.region_1.2_spmd.sunk | while | flops 100360 | bytes 1706193 | solution.py:148
  187.6 1.3 collective-permute-start.4
  188.9 1.3 collective-permute-start.5
  190.2 4.3 %collective-permute-done.5 = bf16[1,32,256]{2,0,1:T(2,128)(2,1)S(1)} collective-permute-done((bf16[1,32,256]{2,0,1:T(2,128)(2,1)S(1)}, bf16[1,32,256]{2,0,1:T(2,128)(2,1)S(1)}, u32[]{:S(2)}, u32[]{:S(2)}) %collective-permute-start.5) | collective-permute-done | bytes 16416 | tf_op jit(solution)/shard_map/ppermute | solution.py:18
  194.6 1.8 collective-permute-start.6
  196.4 1.3 collective-permute-start.7
  197.8 4.2 %collective-permute-done.7 = bf16[18,1,256]{2,0,1:T(8,128)(2,1)S(1)} collective-permute-done((bf16[18,1,256]{2,0,1:T(8,128)(2,1)S(1)}, bf16[18,1,256]{2,0,1:T(8,128)(2,1)S(1)}, u32[]{:S(2)}, u32[]{:S(2)}) %collective-permute-start.7) | collective-permute-done | bytes 9248 | tf_op jit(solution)/shard_map/ppermute | solution.py:18
  204.3 80.6 %all-reduce.5.cloned.1.call-done = (f32[3,3,256,256]{3,2,1,0:T(8,128)}, f32[3,3,256,256]{3,2,1,0:T(8,128)}) async-done(((f32[3,3,256,256]{3,2,1,0:T(8,128)}, f32[3,3,256,256]{3,2,1,0:T(8,128)}), (f32[3,3,256,256]{3,2,1,0:T(8,128)}, f32[3,3,256,256]{3,2,1,0:T(8,128)})) %all-reduce.5.cloned.1.call-update) | async-done | bytes 4718608 | tf_op jit(solution)/shard_map/psum | solution.py:136
  284.9 3.4 %broadcast_multiply_fusion.1 = f32[3,3,256,256]{3,2,1,0:T(8,128)} fusion(f32[3,3,256,256]{3,2,1,0:T(8,128)} %get-tuple-element.153), kind=kLoop, calls=%fused_computation.29 | loop fusion | flops 589824 | bytes 4718592 | tf_op jit(solution)/shard_map/mul | solution.py:154
  288.3 1.6 broadcast_multiply_fusion
  (196 shorter events, 53.8 us)
Async XLA Ops:
  7.2 49.2 %copy-start = (bf16[3,3,256,256]{3,2,1,0:T(8,128)(2,1)S(1)}, bf16[3,3,256,256]{3,2,1,0:T(8,128)(2,1)}, u32[]{:S(2)}) copy-start(bf16[3,3,256,256]{3,2,1,0:T(8,128)(2,1)} %param.11) | copy-start | bytes 3538948
  8.0 8.8 %collective-permute-start.1 = (bf16[1,32,256]{2,1,0:T(8,128)(2,1)S(1)}, bf16[1,32,256]{2,1,0:T(8,128)(2,1)S(1)}, u32[]{:S(2)}, u32[]{:S(2)}) collective-permute-start(bf16[1,32,256]{2,1,0:T(8,128)(2,1)S(1)} %get-tuple-element.173), channel_id=1, source_target_pairs={{4,0},{8,4},{12,8},{16,12},{20,16},{24,20},{28,24},{5,1},{9,5},{13... | collective-permute-start | bytes 49160 | tf_op jit(solution)/shard_map/ppermute | solution.py:18
  9.3 6.6 %collective-permute-start = (bf16[1,32,256]{2,1,0:T(8,128)(2,1)S(1)}, bf16[1,32,256]{2,1,0:T(8,128)(2,1)S(1)}, u32[]{:S(2)}, u32[]{:S(2)}) collective-permute-start(bf16[1,32,256]{2,1,0:T(8,128)(2,1)S(1)} %get-tuple-element.174), channel_id=1, source_target_pairs={{0,4},{4,8},{8,12},{12,16},{16,20},{20,24},{24,28},{1,5},{5,9},{9,... | collective-permute-start | bytes 49160 | tf_op jit(solution)/shard_map/ppermute | solution.py:17
  16.9 6.4 %collective-permute-start.2 = (bf16[18,1,256]{2,1,0:T(2,128)(2,1)S(1)}, bf16[18,1,256]{2,1,0:T(2,128)(2,1)S(1)}, u32[]{:S(2)}, u32[]{:S(2)}) collective-permute-start(bf16[18,1,256]{2,1,0:T(2,128)(2,1)S(1)} %get-tuple-element.169), channel_id=1, source_target_pairs={{0,1},{1,2},{2,3},{4,5},{5,6},{6,7},{8,9},{9,10},{10,11},{12,13},{... | collective-permute-start | bytes 27656 | tf_op jit(solution)/shard_map/ppermute | solution.py:17
  21.9 5.7 %collective-permute-start.3 = (bf16[18,1,256]{2,1,0:T(2,128)(2,1)S(1)}, bf16[18,1,256]{2,1,0:T(2,128)(2,1)S(1)}, u32[]{:S(2)}, u32[]{:S(2)}) collective-permute-start(bf16[18,1,256]{2,1,0:T(2,128)(2,1)S(1)} %get-tuple-element.170), channel_id=1, source_target_pairs={{1,0},{2,1},{3,2},{5,4},{6,5},{7,6},{9,8},{10,9},{11,10},{13,12},{... | collective-permute-start | bytes 27656 | tf_op jit(solution)/shard_map/ppermute | solution.py:18
  50.0 5.2 %copy-start.19 = (s32[8,1]{0,1:T(1,128)S(1)}, s32[8,1]{0,1:T(1,128)}, u32[]{:S(2)}) copy-start(s32[8,1]{0,1:T(1,128)} %param.16) | copy-start | bytes 100
  51.2 5.2 %copy-start.20 = (pred[8,5]{0,1:T(8,128)(4,1)S(1)}, pred[8,5]{0,1:T(8,128)(4,1)}, u32[]{:S(2)}) copy-start(pred[8,5]{0,1:T(8,128)(4,1)} %constant.129) | copy-start | bytes 124
  51.2 29.9 %all-to-all-start.1 = ((bf16[4,2,16,16,256]{4,3,2,1,0:T(8,128)(2,1)}), bf16[4,2,16,16,256]{4,3,2,1,0:T(8,128)(2,1)S(1)}, u32[]{:S(2)}, u32[]{:S(2)}) async-start(bf16[4,2,16,16,256]{4,3,2,1,0:T(8,128)(2,1)} %bitcast.140), calls=%async_computation.1 | async-start | bytes 2097152 | tf_op jit(solution)/shard_map/all_to_all | solution.py:109
  81.0 8.7 %all-to-all-start = ((bf16[4,2,4]{2,1,0:T(2,128)(2,1)}), bf16[4,2,4]{2,1,0:T(2,128)(2,1)S(1)}, u32[]{:S(2)}, u32[]{:S(2)}) async-start(bf16[4,2,4]{2,1,0:T(2,128)(2,1)} %bitcast.9), calls=%async_computation | async-start | bytes 4096 | tf_op jit(solution)/shard_map/all_to_all | solution.py:110
  90.2 0.7 copy-start.14
  92.2 1.3 copy-start.18
  94.7 1.2 copy-start.8
  94.7 1.8 copy-start.17
  100.3 0.8 copy-start.6
  105.3 6.1 %copy-start.4 = (bf16[14,4,16,256]{3,2,1,0:T(8,128)(2,1)}, bf16[14,4,16,256]{3,2,1,0:T(8,128)(2,1)S(1)}, u32[]{:S(2)}) copy-start(bf16[14,4,16,256]{3,2,1,0:T(8,128)(2,1)S(1)} %reshape.159) | copy-start | bytes 1376260
  116.3 5.3 %copy-start.10 = (bf16[4,14,14,256]{3,2,1,0:T(8,128)(2,1)S(1)}, bf16[4,14,14,256]{3,2,1,0:T(8,128)(2,1)}, u32[]{:S(2)}) copy-start(bf16[4,14,14,256]{3,2,1,0:T(8,128)(2,1)} %copy_bitcast_fusion.2) | copy-start | bytes 1204228
  118.1 22.3 %all-to-all-start.2 = ((bf16[4,2,14,14,256]{4,1,3,2,0:T(2,128)(2,1)}), bf16[4,2,14,14,256]{4,1,3,2,0:T(2,128)(2,1)S(1)}, u32[]{:S(2)}, u32[]{:S(2)}) async-start(bf16[4,2,14,14,256]{4,1,3,2,0:T(2,128)(2,1)} %copy.105), calls=%async_computation.2 | async-start | bytes 1605632 | tf_op jit(solution)/shard_map/all_to_all | solution.py:131
  121.6 1.5 copy-start.12
  121.6 163.3 %all-reduce.5.cloned.1.call-start = ((), (), s32[]{:S(2)}) async-start(), calls=%async_computation.3 | async-start | bytes 9437184 | tf_op jit(solution)/shard_map/psum | solution.py:136
  123.4 1.0 copy-start.13
  124.5 1.0 copy-start.5
  126.2 1.0 copy-start.11
  127.2 1.0 copy-start.7
  127.2 1.2 copy-start.9
  134.0 1.5 copy-start.2
  140.6 1.3 copy-start.15
  140.6 1.3 copy-start.16
  141.9 45.5 %copy-start.3 = (f32[16,8,5,256]{3,0,2,1:T(8,128)S(1)}, f32[16,8,5,256]{3,0,2,1:T(8,128)}, u32[]{:S(2)}) copy-start(f32[16,8,5,256]{3,0,2,1:T(8,128)} %copy.111) | copy-start | bytes 1966084
  187.6 2.6 collective-permute-start.4
  188.9 5.6 %collective-permute-start.5 = (bf16[1,32,256]{2,0,1:T(2,128)(2,1)S(1)}, bf16[1,32,256]{2,0,1:T(2,128)(2,1)S(1)}, u32[]{:S(2)}, u32[]{:S(2)}) collective-permute-start(bf16[1,32,256]{2,0,1:T(2,128)(2,1)S(1)} %get-tuple-element.172), channel_id=1, source_target_pairs={{4,0},{8,4},{12,8},{16,12},{20,16},{24,20},{28,24},{5,1},{9,5},{13... | collective-permute-start | bytes 49160 | tf_op jit(solution)/shard_map/ppermute | solution.py:18
  194.6 3.2 %collective-permute-start.6 = (bf16[18,1,256]{2,0,1:T(8,128)(2,1)S(1)}, bf16[18,1,256]{2,0,1:T(8,128)(2,1)S(1)}, u32[]{:S(2)}, u32[]{:S(2)}) collective-permute-start(bf16[18,1,256]{2,0,1:T(8,128)(2,1)S(1)} %get-tuple-element.167), channel_id=1, source_target_pairs={{0,1},{1,2},{2,3},{4,5},{5,6},{6,7},{8,9},{9,10},{10,11},{12,13},{... | collective-permute-start | bytes 27656 | tf_op jit(solution)/shard_map/ppermute | solution.py:17
  196.4 5.6 %collective-permute-start.7 = (bf16[18,1,256]{2,0,1:T(8,128)(2,1)S(1)}, bf16[18,1,256]{2,0,1:T(8,128)(2,1)S(1)}, u32[]{:S(2)}, u32[]{:S(2)}) collective-permute-start(bf16[18,1,256]{2,0,1:T(8,128)(2,1)S(1)} %get-tuple-element.168), channel_id=1, source_target_pairs={{1,0},{2,1},{3,2},{5,4},{6,5},{7,6},{9,8},{10,9},{11,10},{13,12},{... | collective-permute-start | bytes 27656 | tf_op jit(solution)/shard_map/ppermute | solution.py:18
  284.9 3.4 %copy-start.1 = (f32[3,3,256,256]{3,2,1,0:T(8,128)S(1)}, f32[3,3,256,256]{3,2,1,0:T(8,128)}, u32[]{:S(2)}) copy-start(f32[3,3,256,256]{3,2,1,0:T(8,128)} %get-tuple-element.154) | copy-start | bytes 7077892
Sparse Core Ops, SparseCore 0:
  138.8 146.0 all-reduce.4
where the time goes:
time: 298 us; the launch traced here: 297 us
  waiting for transfers between devices  123 us (41%)
  local copies, waits for them, and re-layouts  60.4 us (20%)
  loops' own time  31.5 us (11%)
  starting transfers between devices  27.2 us (9%)
  matrix products  27.2 us (9%)
  between operations  14.9 us (5%)
  other arithmetic  12.8 us (4%)
    psum x1, waiting for transfers between devices, body(): lax.psum((first_local, second_local), ('row', 'col'))  80.6 us
    another operation x1, loops' own time, body(): lax.fori_loop(0, slot_count, add_box, jnp.zeros((tile_rows, tile_cols, ch...  31.5 us
    all_to_all x1, waiting for transfers between devices, body(): lax.all_to_all(outgoing, 'col', split_axis=0, concat_axis=0, tiled=True)  22.7 us
    gather x24, local copies, waits for them, and re-layouts  19.9 us
    dot_general x18, matrix products, weight_grad(): lax.dot_general(window, flat_delta, (((0,), (0,)), ((), ())), preferred_e...  14 us
    ppermute x4, waiting for transfers between devices, padded_2(): after = lax.ppermute(leading, axis, down)  12.8 us
    ppermute x4, starting transfers between devices, padded_2(): before = lax.ppermute(last, axis, up)  11.1 us
    conv_general_dilated x7, matrix products, conv_pad(): lax.conv_general_dilated(inputs, kernel, (1, 1), ((margin, margin), (marg...  11.1 us
  transfers between devices with their start and end apart: 12, of which 9 were waited for; matrix products, arithmetic and copies ran while one was open for 13% of the time, Pallas kernels for 0%

commit v1 on v0

--- a/solution.py
+++ b/solution.py
@@ -71,6 +71,29 @@
 
 
 def body(in_map, tile_w, head_w1, head_w2, box_row, box_col, box_target, head_cot):
+
+    def waves_assign(chip_axis, block_in, array_axis, pos_dim):
+        z = lax.axis_size(chip_axis)
+        a_next = lax.axis_index(chip_axis)
+        later, z1 = (z, a_next)
+        high = block_in.shape[array_axis] // later
+        side_arr = list(block_in.shape)
+        side_arr[array_axis] = high
+        back = side_arr[pos_dim]
+        side_arr[pos_dim] = back * later
+        all_rows = jnp.zeros(side_arr, block_in.dtype)
+        for w in range(later):
+            all_values = lax.dynamic_slice_in_dim(block_in, (z1 ^ w) * high, high, axis=array_axis)
+            if w:
+                z_new = range(later)
+                v_next = map(lambda k: (k, k ^ w), z_new)
+                h_now = list(v_next)
+                all_values = lax.ppermute(all_values, axis_name=chip_axis, perm=h_now)
+            all_rows = lax.dynamic_update_slice_in_dim(
+                all_rows, all_values, (z1 ^ w) * back, axis=pos_dim
+            )
+        return all_rows
+
     tile_rows, tile_cols, channels = in_map.shape
     head_count = head_cot.shape[0]
     box_side = head_cot.shape[2]
@@ -106,7 +129,7 @@
     )(top_row, left_col)
     outgoing = pick_rows(send_map, windows).reshape(columns, capacity, window, window, channels)
     arrived, arrived_head = (
-        lax.all_to_all(outgoing, "col", split_axis=0, concat_axis=0, tiled=True),
+        waves_assign("col", outgoing, 0, pos_dim=0),
         lax.all_to_all(pair_head, "col", split_axis=0, concat_axis=0, tiled=True),
     )
     arrived_head = arrived_head.reshape(pair_count, head_count)

time: 298 us -> 287 us (0.963)
  waiting for transfers between devices: 123 us -> 115 us
  local copies, waits for them, and re-layouts: 60.4 us -> 54.1 us
    all_to_all x1 -> x0, waiting for transfers between devices: 22.7 us -> none  [body(): lax.all_to_all(outgoing, 'col', split_axis=0, concat_axis=0, tiled=True)]
    ppermute x0 -> x3, waiting for transfers between devices: none -> 19.6 us  [waves_assign(): all_values = lax.ppermute(all_values, axis_name=chip_axis, perm=h_now)]
    all_to_all x1, waiting for transfers between devices: 4.8 us -> 0.01 us  [body(): lax.all_to_all(pair_head, 'col', split_axis=0, concat_axis=0, tiled=True)]
    ppermute x0 -> x3, starting transfers between devices: none -> 4.45 us  [waves_assign(): all_values = lax.ppermute(all_values, axis_name=chip_axis, perm=h_now)]
    gather x24, local copies, waits for them, and re-layouts: 19.9 us -> 15.6 us
    all_to_all x1 -> x0, starting transfers between devices: 3.99 us -> none  [body(): lax.all_to_all(outgoing, 'col', split_axis=0, concat_axis=0, tiled=True)]
    unnamed x49 -> x47, local copies, waits for them, and re-layouts: 9.91 us -> 7.71 us
  transfers between devices with their start and end apart: 12 -> 14, of which waited for: 9 -> 10; matrix products, arithmetic and copies ran while one was open for 13% -> 19% of each run, Pallas kernels for 0% -> 0%
where the time goes in v1:
time: 287 us; the launch traced here: 285 us
  waiting for transfers between devices  115 us (40%)
  local copies, waits for them, and re-layouts  54.1 us (19%)
  loops' own time  31.7 us (11%)
  starting transfers between devices  29.1 us (10%)
  matrix products  27 us (9%)
  between operations  14.9 us (5%)
  other arithmetic  13.5 us (5%)
    psum x1, waiting for transfers between devices, body(): lax.psum((first_local, second_local), ('row', 'col'))  79.8 us
    another operation x1, loops' own time, body(): lax.fori_loop(0, slot_count, add_box, jnp.zeros((tile_rows, tile_cols, ch...  31.5 us
    ppermute x3, waiting for transfers between devices, waves_assign(): all_values = lax.ppermute(all_values, axis_name=chip_axis, perm=h_now)  19.6 us
    gather x24, local copies, waits for them, and re-layouts  15.6 us
    dot_general x18, matrix products, weight_grad(): lax.dot_general(window, flat_delta, (((0,), (0,)), ((), ())), preferred_e...  14 us
    ppermute x4, waiting for transfers between devices, padded_2(): after = lax.ppermute(leading, axis, down)  11.8 us
    conv_general_dilated x7, matrix products, conv_pad(): lax.conv_general_dilated(inputs, kernel, (1, 1), ((margin, margin), (marg...  11.1 us
    ppermute x4, starting transfers between devices, padded_2(): before = lax.ppermute(last, axis, up)  9.54 us
  transfers between devices with their start and end apart: 14, of which 10 were waited for; matrix products, arithmetic and copies ran while one was open for 19% of the time, Pallas kernels for 0%

profile of v1, /device:TPU:0, one launch (start us, length us, event | category | flops | bytes accessed | tf_op | source)
XLA Modules:
  0.0 285.5 jit_solution(9142593517253688962)
XLA Ops:
  11.7 6.3 %all-to-all-start = ((bf16[4,2,4]{2,1,0:T(2,128)(2,1)}), bf16[4,2,4]{2,1,0:T(2,128)(2,1)S(1)}, u32[]{:S(2)}, u32[]{:S(2)}) async-start(bf16[4,2,4]{2,1,0:T(2,128)(2,1)} %bitcast.9), calls=%async_computation | async-start | bytes 4096 | tf_op jit(solution)/shard_map/all_to_all | solution.py:133
  18.8 1.3 collective-permute-start.1
  20.1 3.0 %collective-permute-start = (bf16[1,32,256]{2,1,0:T(8,128)(2,1)S(1)}, bf16[1,32,256]{2,1,0:T(8,128)(2,1)S(1)}, u32[]{:S(2)}, u32[]{:S(2)}) collective-permute-start(bf16[1,32,256]{2,1,0:T(8,128)(2,1)S(1)} %get-tuple-element.178), channel_id=1, source_target_pairs={{0,4},{4,8},{8,12},{12,16},{16,20},{20,24},{24,28},{1,5},{5,9},{9,... | collective-permute-start | bytes 49160 | tf_op jit(solution)/shard_map/ppermute | solution.py:17
  25.0 3.9 %collective-permute-start.2 = (bf16[18,1,256]{2,1,0:T(2,128)(2,1)S(1)}, bf16[18,1,256]{2,1,0:T(2,128)(2,1)S(1)}, u32[]{:S(2)}, u32[]{:S(2)}) collective-permute-start(bf16[18,1,256]{2,1,0:T(2,128)(2,1)S(1)} %get-tuple-element.173), channel_id=1, source_target_pairs={{0,1},{1,2},{2,3},{4,5},{5,6},{6,7},{8,9},{9,10},{10,11},{12,13},{... | collective-permute-start | bytes 27656 | tf_op jit(solution)/shard_map/ppermute | solution.py:17
  28.9 1.3 collective-permute-start.3
  30.4 4.3 %collective-permute-done.3 = bf16[18,1,256]{2,1,0:T(2,128)(2,1)S(1)} collective-permute-done((bf16[18,1,256]{2,1,0:T(2,128)(2,1)S(1)}, bf16[18,1,256]{2,1,0:T(2,128)(2,1)S(1)}, u32[]{:S(2)}, u32[]{:S(2)}) %collective-permute-start.3) | collective-permute-done | bytes 9248 | tf_op jit(solution)/shard_map/ppermute | solution.py:18
  35.1 15.8 %while.15 = (s32[]{:T(128)}, bf16[18,34,256]{2,1,0:T(8,128)(2,1)S(1)}, s32[8,3]{0,1:T(4,128)S(1)}, bf16[8,16,16,256]{3,2,1,0:T(8,128)(2,1)S(1)}, s32[]{:T(128)}) while((s32[]{:T(128)}, bf16[18,34,256]{2,1,0:T(8,128)(2,1)S(1)}, s32[8,3]{0,1:T(4,128)S(1)}, bf16[8,16,16,256]{3,2,1,0:T(8,128)(2,1)S(1)}, s32[]{:T(128)}) %tuple.67), condition=%wide.while_cond, body=%wide.while_body.sunk | while | flops 2 | bytes 262269 | solution.py:128
  35.7 1.3 bitcast_dynamic-update-slice_fusion.2
  37.7 1.3 bitcast_dynamic-update-slice_fusion.2
  39.7 1.3 bitcast_dynamic-update-slice_fusion.2
  41.6 1.3 bitcast_dynamic-update-slice_fusion.2
  43.6 1.3 bitcast_dynamic-update-slice_fusion.2
  45.6 1.3 bitcast_dynamic-update-slice_fusion.2
  47.6 1.3 bitcast_dynamic-update-slice_fusion.2
  49.5 1.3 bitcast_dynamic-update-slice_fusion.2
  52.3 1.5 collective-permute-start.6
  53.8 1.5 collective-permute-start.5
  55.3 1.5 collective-permute-start.4
  57.7 1.1 copy.111
  58.8 12.1 %collective-permute-done.4 = bf16[1,2,16,16,256]{4,3,2,1,0:T(8,128)(2,1)S(1)} collective-permute-done((bf16[1,2,16,16,256]{4,3,2,1,0:T(8,128)(2,1)S(1)}, bf16[1,2,16,16,256]{4,3,2,1,0:T(8,128)(2,1)S(1)}, u32[]{:S(2)}, u32[]{:S(2)}) %collective-permute-start.4) | collective-permute-done | bytes 262176 | tf_op jit(solution)/shard_map/ppermute | solution.py:91
  70.9 7.4 %collective-permute-done.5 = bf16[1,2,16,16,256]{4,3,2,1,0:T(8,128)(2,1)S(1)} collective-permute-done((bf16[1,2,16,16,256]{4,3,2,1,0:T(8,128)(2,1)S(1)}, bf16[1,2,16,16,256]{4,3,2,1,0:T(8,128)(2,1)S(1)}, u32[]{:S(2)}, u32[]{:S(2)}) %collective-permute-start.5) | collective-permute-done | bytes 262176 | tf_op jit(solution)/shard_map/ppermute | solution.py:91
  80.1 1.3 multiply_convert_fusion.1
  82.6 1.2 fusion.43
  83.9 1.1 select_bitcast_fusion.1
  85.6 1.3 add_multiply_fusion
  88.3 1.2 fusion.62
  90.8 2.9 %fusion.9 = bf16[14,32,2,256]{3,1,2,0:T(8,128)(2,1)S(1)} fusion(bf16[3,3,256,256]{3,2,1,0:T(8,128)(2,1)} %param.13, bf16[14,4,7,2,256]{4,2,1,3,0:T(8,128)(2,1)S(1)} %slice.138, bf16[14,4,8,2,256]{4,2,1,3,0:T(8,128)(2,1)S(1)} %copy.102, f32[14,32,2,256]{3,1,2,0:T(8,128)} %copy-done.8, pred[32,2]{0,1:T(4,128)(4,1)S(1)} %copy-done.14), kind=kOutput, calls=%fused_computation.23 | convolution fusion | flops 1011679232 | bytes 3416128 | tf_op jit(solution)/shard_map/conv_general_dilated | solution.py:24
  95.3 2.4 copy.120
  97.8 1.2 reshape.164
  100.8 2.5 convolution_convert_fusion.4
  105.4 1.8 copy.105
  107.2 3.6 %all-to-all-start.1 = ((bf16[4,2,14,14,256]{4,1,3,2,0:T(2,128)(2,1)}), bf16[4,2,14,14,256]{4,1,3,2,0:T(2,128)(2,1)S(1)}, u32[]{:S(2)}, u32[]{:S(2)}) async-start(bf16[4,2,14,14,256]{4,1,3,2,0:T(2,128)(2,1)} %copy.105), calls=%async_computation.1 | async-start | bytes 1605632 | tf_op jit(solution)/shard_map/all_to_all | solution.py:154
  110.8 1.4 fusion.28
  119.6 1.1 fusion.17
  123.2 1.3 fusion.14
  124.6 1.1 fusion.13
  125.7 1.1 fusion.12
  127.8 3.6 %all-to-all-done.1 = bf16[4,2,14,14,256]{4,1,3,2,0:T(2,128)(2,1)S(1)} async-done(((bf16[4,2,14,14,256]{4,1,3,2,0:T(2,128)(2,1)}), bf16[4,2,14,14,256]{4,1,3,2,0:T(2,128)(2,1)S(1)}, u32[]{:S(2)}, u32[]{:S(2)}) %all-to-all-start.1) | async-done | bytes 802848 | tf_op jit(solution)/shard_map/all_to_all | solution.py:154
  132.9 45.5 %while.14 = (s32[]{:T(128)}, f32[16,32,256]{2,0,1:T(8,128)S(1)}, s32[8]{0:T(128)S(1)}, s32[8]{0:T(128)S(1)}, bf16[8,14,14,256]{3,2,1,0:T(8,128)(2,1)S(1)}, /*index=5*/s32[]{:T(128)}, s32[]{:T(128)}, s32[]{:T(128)}, s32[]{:T(128)}) while((s32[]{:T(128)}, f32[16,32,256]{2,0,1:T(8,128)S(1)}, s32[8]{0:T(128)S(1)}, s32[8]{0:T(128)S(1)}, ...), condition=%wide.region_2.3_spmd, body=%wide.region_1.2_spmd.sunk | while | flops 100360 | bytes 1706193 | solution.py:171
  178.7 1.3 collective-permute-start.7
  180.0 1.3 collective-permute-start.8
  181.3 3.1 %collective-permute-done.8 = bf16[1,32,256]{2,0,1:T(2,128)(2,1)S(1)} collective-permute-done((bf16[1,32,256]{2,0,1:T(2,128)(2,1)S(1)}, bf16[1,32,256]{2,0,1:T(2,128)(2,1)S(1)}, u32[]{:S(2)}, u32[]{:S(2)}) %collective-permute-start.8) | collective-permute-done | bytes 16416 | tf_op jit(solution)/shard_map/ppermute | solution.py:18
  184.4 1.3 collective-permute-start.9
  185.7 1.3 collective-permute-start.10
  187.1 4.4 %collective-permute-done.10 = bf16[18,1,256]{2,0,1:T(8,128)(2,1)S(1)} collective-permute-done((bf16[18,1,256]{2,0,1:T(8,128)(2,1)S(1)}, bf16[18,1,256]{2,0,1:T(8,128)(2,1)S(1)}, u32[]{:S(2)}, u32[]{:S(2)}) %collective-permute-start.10) | collective-permute-done | bytes 9248 | tf_op jit(solution)/shard_map/ppermute | solution.py:18
  193.8 79.8 %all-reduce.5.cloned.1.call-done = (f32[3,3,256,256]{3,2,1,0:T(8,128)}, f32[3,3,256,256]{3,2,1,0:T(8,128)}) async-done(((f32[3,3,256,256]{3,2,1,0:T(8,128)}, f32[3,3,256,256]{3,2,1,0:T(8,128)}), (f32[3,3,256,256]{3,2,1,0:T(8,128)}, f32[3,3,256,256]{3,2,1,0:T(8,128)})) %all-reduce.5.cloned.1.call-update) | async-done | bytes 4718608 | tf_op jit(solution)/shard_map/psum | solution.py:159
  273.6 3.4 %broadcast_multiply_fusion.1 = f32[3,3,256,256]{3,2,1,0:T(8,128)} fusion(f32[3,3,256,256]{3,2,1,0:T(8,128)} %get-tuple-element.153), kind=kLoop, calls=%fused_computation.29 | loop fusion | flops 589824 | bytes 4718592 | tf_op jit(solution)/shard_map/mul | solution.py:177
  277.0 1.6 broadcast_multiply_fusion
  (203 shorter events, 55.5 us)
Async XLA Ops:
  7.2 49.6 %copy-start = (bf16[3,3,256,256]{3,2,1,0:T(8,128)(2,1)S(1)}, bf16[3,3,256,256]{3,2,1,0:T(8,128)(2,1)}, u32[]{:S(2)}) copy-start(bf16[3,3,256,256]{3,2,1,0:T(8,128)(2,1)} %param.11) | copy-start | bytes 3538948
  11.7 67.2 %all-to-all-start = ((bf16[4,2,4]{2,1,0:T(2,128)(2,1)}), bf16[4,2,4]{2,1,0:T(2,128)(2,1)S(1)}, u32[]{:S(2)}, u32[]{:S(2)}) async-start(bf16[4,2,4]{2,1,0:T(2,128)(2,1)} %bitcast.9), calls=%async_computation | async-start | bytes 4096 | tf_op jit(solution)/shard_map/all_to_all | solution.py:133
  18.8 6.1 %collective-permute-start.1 = (bf16[1,32,256]{2,1,0:T(8,128)(2,1)S(1)}, bf16[1,32,256]{2,1,0:T(8,128)(2,1)S(1)}, u32[]{:S(2)}, u32[]{:S(2)}) collective-permute-start(bf16[1,32,256]{2,1,0:T(8,128)(2,1)S(1)} %get-tuple-element.177), channel_id=1, source_target_pairs={{4,0},{8,4},{12,8},{16,12},{20,16},{24,20},{28,24},{5,1},{9,5},{13... | collective-permute-start | bytes 49160 | tf_op jit(solution)/shard_map/ppermute | solution.py:18
  20.1 3.9 %collective-permute-start = (bf16[1,32,256]{2,1,0:T(8,128)(2,1)S(1)}, bf16[1,32,256]{2,1,0:T(8,128)(2,1)S(1)}, u32[]{:S(2)}, u32[]{:S(2)}) collective-permute-start(bf16[1,32,256]{2,1,0:T(8,128)(2,1)S(1)} %get-tuple-element.178), channel_id=1, source_target_pairs={{0,4},{4,8},{8,12},{12,16},{16,20},{20,24},{24,28},{1,5},{5,9},{9,... | collective-permute-start | bytes 49160 | tf_op jit(solution)/shard_map/ppermute | solution.py:17
  25.0 5.4 %collective-permute-start.2 = (bf16[18,1,256]{2,1,0:T(2,128)(2,1)S(1)}, bf16[18,1,256]{2,1,0:T(2,128)(2,1)S(1)}, u32[]{:S(2)}, u32[]{:S(2)}) collective-permute-start(bf16[18,1,256]{2,1,0:T(2,128)(2,1)S(1)} %get-tuple-element.173), channel_id=1, source_target_pairs={{0,1},{1,2},{2,3},{4,5},{5,6},{6,7},{8,9},{9,10},{10,11},{12,13},{... | collective-permute-start | bytes 27656 | tf_op jit(solution)/shard_map/ppermute | solution.py:17
  28.9 5.7 %collective-permute-start.3 = (bf16[18,1,256]{2,1,0:T(2,128)(2,1)S(1)}, bf16[18,1,256]{2,1,0:T(2,128)(2,1)S(1)}, u32[]{:S(2)}, u32[]{:S(2)}) collective-permute-start(bf16[18,1,256]{2,1,0:T(2,128)(2,1)S(1)} %get-tuple-element.174), channel_id=1, source_target_pairs={{1,0},{2,1},{3,2},{5,4},{6,5},{7,6},{9,8},{10,9},{11,10},{13,12},{... | collective-permute-start | bytes 27656 | tf_op jit(solution)/shard_map/ppermute | solution.py:18
  51.9 4.9 %copy-start.19 = (pred[8,5]{0,1:T(8,128)(4,1)S(1)}, pred[8,5]{0,1:T(8,128)(4,1)}, u32[]{:S(2)}) copy-start(pred[8,5]{0,1:T(8,128)(4,1)} %constant.137) | copy-start | bytes 124
  52.3 26.1 %collective-permute-start.6 = (bf16[1,2,16,16,256]{4,3,2,1,0:T(8,128)(2,1)S(1)}, bf16[1,2,16,16,256]{4,3,2,1,0:T(8,128)(2,1)S(1)}, u32[]{:S(2)}, u32[]{:S(2)}) collective-permute-start(bf16[1,2,16,16,256]{4,3,2,1,0:T(8,128)(2,1)S(1)} %get-tuple-element.159), channel_id=1, source_target_pairs={{0,3},{1,2},{2,1},{3,0},{4,7},{5,6},{6,5},{7,4},{8,11},{9,10},{10,... | collective-permute-start | bytes 786440 | tf_op jit(solution)/shard_map/ppermute | solution.py:91
  53.8 24.5 %collective-permute-start.5 = (bf16[1,2,16,16,256]{4,3,2,1,0:T(8,128)(2,1)S(1)}, bf16[1,2,16,16,256]{4,3,2,1,0:T(8,128)(2,1)S(1)}, u32[]{:S(2)}, u32[]{:S(2)}) collective-permute-start(bf16[1,2,16,16,256]{4,3,2,1,0:T(8,128)(2,1)S(1)} %get-tuple-element.160), channel_id=1, source_target_pairs={{0,2},{1,3},{2,0},{3,1},{4,6},{5,7},{6,4},{7,5},{8,10},{9,11},{10,... | collective-permute-start | bytes 786440 | tf_op jit(solution)/shard_map/ppermute | solution.py:91
  55.3 15.6 %collective-permute-start.4 = (bf16[1,2,16,16,256]{4,3,2,1,0:T(8,128)(2,1)S(1)}, bf16[1,2,16,16,256]{4,3,2,1,0:T(8,128)(2,1)S(1)}, u32[]{:S(2)}, u32[]{:S(2)}) collective-permute-start(bf16[1,2,16,16,256]{4,3,2,1,0:T(8,128)(2,1)S(1)} %get-tuple-element.161), channel_id=1, source_target_pairs={{0,1},{1,0},{2,3},{3,2},{4,5},{5,4},{6,7},{7,6},{8,9},{9,8},{10,11... | collective-permute-start | bytes 786440 | tf_op jit(solution)/shard_map/ppermute | solution.py:91
  79.4 0.7 copy-start.14
  81.3 1.3 copy-start.18
  83.8 1.2 copy-start.8
  83.8 1.8 copy-start.17
  89.4 0.8 copy-start.6
  94.4 6.3 %copy-start.4 = (bf16[14,4,16,256]{3,2,1,0:T(8,128)(2,1)}, bf16[14,4,16,256]{3,2,1,0:T(8,128)(2,1)S(1)}, u32[]{:S(2)}) copy-start(bf16[14,4,16,256]{3,2,1,0:T(8,128)(2,1)S(1)} %reshape.159) | copy-start | bytes 1376260
  105.4 5.4 %copy-start.10 = (bf16[4,14,14,256]{3,2,1,0:T(8,128)(2,1)S(1)}, bf16[4,14,14,256]{3,2,1,0:T(8,128)(2,1)}, u32[]{:S(2)}) copy-start(bf16[4,14,14,256]{3,2,1,0:T(8,128)(2,1)} %copy_bitcast_fusion.2) | copy-start | bytes 1204228
  107.2 24.3 %all-to-all-start.1 = ((bf16[4,2,14,14,256]{4,1,3,2,0:T(2,128)(2,1)}), bf16[4,2,14,14,256]{4,1,3,2,0:T(2,128)(2,1)S(1)}, u32[]{:S(2)}, u32[]{:S(2)}) async-start(bf16[4,2,14,14,256]{4,1,3,2,0:T(2,128)(2,1)} %copy.105), calls=%async_computation.1 | async-start | bytes 1605632 | tf_op jit(solution)/shard_map/all_to_all | solution.py:154
  110.8 1.4 copy-start.12
  110.8 162.8 %all-reduce.5.cloned.1.call-start = ((), (), s32[]{:S(2)}) async-start(), calls=%async_computation.2 | async-start | bytes 9437184 | tf_op jit(solution)/shard_map/psum | solution.py:159
  112.6 1.0 copy-start.13
  113.6 1.0 copy-start.5
  115.4 1.0 copy-start.11
  116.4 1.0 copy-start.7
  116.4 1.2 copy-start.9
  123.1 1.5 copy-start.2
  131.6 1.3 copy-start.15
  131.6 1.3 copy-start.16
  132.9 45.5 %copy-start.3 = (f32[16,8,5,256]{3,0,2,1:T(8,128)S(1)}, f32[16,8,5,256]{3,0,2,1:T(8,128)}, u32[]{:S(2)}) copy-start(f32[16,8,5,256]{3,0,2,1:T(8,128)} %copy.111) | copy-start | bytes 1966084
  178.7 2.6 collective-permute-start.7
  180.0 4.4 %collective-permute-start.8 = (bf16[1,32,256]{2,0,1:T(2,128)(2,1)S(1)}, bf16[1,32,256]{2,0,1:T(2,128)(2,1)S(1)}, u32[]{:S(2)}, u32[]{:S(2)}) collective-permute-start(bf16[1,32,256]{2,0,1:T(2,128)(2,1)S(1)} %get-tuple-element.176), channel_id=1, source_target_pairs={{4,0},{8,4},{12,8},{16,12},{20,16},{24,20},{28,24},{5,1},{9,5},{13... | collective-permute-start | bytes 49160 | tf_op jit(solution)/shard_map/ppermute | solution.py:18
  184.4 2.7 collective-permute-start.9
  185.7 5.8 %collective-permute-start.10 = (bf16[18,1,256]{2,0,1:T(8,128)(2,1)S(1)}, bf16[18,1,256]{2,0,1:T(8,128)(2,1)S(1)}, u32[]{:S(2)}, u32[]{:S(2)}) collective-permute-start(bf16[18,1,256]{2,0,1:T(8,128)(2,1)S(1)} %get-tuple-element.172), channel_id=1, source_target_pairs={{1,0},{2,1},{3,2},{5,4},{6,5},{7,6},{9,8},{10,9},{11,10},{13,12},{... | collective-permute-start | bytes 27656 | tf_op jit(solution)/shard_map/ppermute | solution.py:18
  273.6 3.4 %copy-start.1 = (f32[3,3,256,256]{3,2,1,0:T(8,128)S(1)}, f32[3,3,256,256]{3,2,1,0:T(8,128)}, u32[]{:S(2)}) copy-start(f32[3,3,256,256]{3,2,1,0:T(8,128)} %get-tuple-element.154) | copy-start | bytes 7077892
Sparse Core Ops, SparseCore 0:
  127.9 145.6 all-reduce.4
